TPU v7x, 256 devices: a whole 4x4x8 slice. The times are simulated.
256 devices in a mesh: group: 32 (over x, y, core), tp: 8 (over z).
Axes of the slice: x: 4, y: 4, z: 8, core: 2. Of those that a mesh axis runs over, the one named last changes fastest.
Arguments:
- hidden_in: bfloat16 [64, 3072], P('group'), may hold values from -6 to 6
- w_qkv: bfloat16 [3072, 2048], P(None, 'tp'), may hold values from -0.109375 to 0.109375
- w_out: bfloat16 [1536, 3072], P('tp'), may hold values from -0.15625 to 0.15625
- kv_pool: bfloat16 [2048, 128, 512], P(('group', 'tp'))
- page_table: int32 [64, 32], replicated, may hold values from 0 to 2047, as said below
- lengths: int32 [64], replicated, may hold values from 1 to 4096, as said below
Outputs:
- attn_proj: bfloat16 [64, 3072], P('group', 'tp')
Inputs may be any that keep to these rules, and one draw needn't show every extreme that they name: `page_table`: every pool slot is named by exactly one request page. `lengths`: some request has the full 32 * 128 cached tokens.
All inputs are finite; a program needn't handle non-finite values.
Results may differ from a plain program's by a relative error of at most 0.0085.
The roundings to bfloat16 on the way count: a program that leaves them out, or rounds other values in their place, can miss the bound.
Values may be sent and summed in bfloat16 or wider, within the bound.
A program may use at most 64 MiB of HBM per device.

v0:
```python
import jax
import jax.numpy as jnp
from jax import lax
from jax.sharding import PartitionSpec as P

HEADS = 12
KV_HEADS = 2
HEAD_DIM = 128


def on_device(hidden_in, w_qkv, w_out, kv_pool, page_table, lengths):
    qdim = HEADS * HEAD_DIM
    kdim = KV_HEADS * HEAD_DIM
    per_kv = HEADS // KV_HEADS
    scale = HEAD_DIM ** (-0.5)
    req_grp = hidden_in.shape[0]
    col_count = w_out.shape[0]
    col_start = lax.axis_index("tp") * col_count
    columns = jnp.dot(hidden_in, w_qkv, preferred_element_type=jnp.float32).astype(jnp.bfloat16)
    qkv = lax.all_gather(columns, "tp", axis=1, tiled=True)
    queries = lax.all_gather(qkv[:, :qdim], "group", axis=0, tiled=True)
    requests = queries.shape[0]
    slot_count = kv_pool.shape[0]
    page_len = kv_pool.shape[1]
    max_pages = page_table.shape[1]
    slot_ids = lax.axis_index(("group", "tp")) * slot_count + jnp.arange(
        slot_count, dtype=jnp.int32
    )
    match = page_table[:, :, None] == slot_ids[None, None, :]
    slot_req = jnp.sum(
        jnp.where(match, jnp.arange(requests, dtype=jnp.int32)[:, None, None], 0), axis=(0, 1)
    )
    slot_page = jnp.sum(
        jnp.where(match, jnp.arange(max_pages, dtype=jnp.int32)[None, :, None], 0), axis=(0, 1)
    )
    chosen = queries[slot_req].reshape(slot_count, KV_HEADS, per_kv, HEAD_DIM)
    keys = kv_pool[..., :kdim].reshape(slot_count, page_len, KV_HEADS, HEAD_DIM)
    values = kv_pool[..., kdim:].reshape(slot_count, page_len, KV_HEADS, HEAD_DIM)
    scores = jnp.einsum("pgjd,ptgd->pgjt", chosen, keys, preferred_element_type=jnp.float32) * scale
    position = slot_page[:, None] * page_len + jnp.arange(page_len, dtype=jnp.int32)[None, :]
    live = (position < lengths[slot_req][:, None])[:, None, None, :]
    top = jnp.max(jnp.where(live, scores, -1e30), axis=-1)
    probs = jnp.where(live, jnp.exp(scores - top[..., None]), 0.0).astype(jnp.bfloat16)
    total = jnp.sum(probs.astype(jnp.float32), axis=-1)
    weighted = jnp.einsum("pgjt,ptgd->pgjd", probs, values, preferred_element_type=jnp.float32)
    owner = slot_req[None, :] == jnp.arange(requests, dtype=jnp.int32)[:, None]
    req_top = jnp.max(jnp.where(owner[:, :, None, None], top[None], -1e30), axis=1)
    factor = jnp.exp(top - req_top[slot_req])
    onehot = owner.astype(jnp.float32)
    req_total = jnp.einsum(
        "rp,pgj->rgj", onehot, total * factor, precision=lax.Precision.HIGHEST
    ).reshape(requests, HEADS)
    req_sums = jnp.einsum(
        "rp,pgjd->rgjd", onehot, weighted * factor[..., None], precision=lax.Precision.HIGHEST
    ).reshape(requests, qdim)
    req_top = req_top.reshape(requests, HEADS)
    start = lax.axis_index("group") * req_grp
    peak_all = lax.pmax(req_top, ("group", "tp"))
    rescale = jnp.exp(req_top - peak_all)
    total_all, sums_all = lax.psum(
        (req_total * rescale, req_sums * jnp.repeat(rescale, HEAD_DIM, axis=1)), ("group", "tp")
    )
    peak = lax.dynamic_slice_in_dim(peak_all, start, req_grp, 0)
    whole = lax.dynamic_slice_in_dim(total_all, start, req_grp, 0)
    sums = lax.dynamic_slice_in_dim(sums_all, start, req_grp, 0)
    sums_part = lax.dynamic_slice_in_dim(sums, col_start, col_count, 1)
    own_q = qkv[:, :qdim].reshape(req_grp, KV_HEADS, per_kv, HEAD_DIM)
    own_k = qkv[:, qdim : qdim + kdim].reshape(req_grp, KV_HEADS, HEAD_DIM)
    own_v = qkv[:, qdim + kdim :].reshape(req_grp, KV_HEADS, HEAD_DIM)
    own_score = (
        jnp.einsum("rgjd,rgd->rgj", own_q, own_k, preferred_element_type=jnp.float32) * scale
    ).reshape(req_grp, HEADS)
    own_sums = jnp.broadcast_to(
        own_v.astype(jnp.float32)[:, :, None, :], (req_grp, KV_HEADS, per_kv, HEAD_DIM)
    ).reshape(req_grp, qdim)
    new_peak = jnp.maximum(peak, own_score)
    old_factor = jnp.exp(peak - new_peak)
    own_factor = jnp.exp(own_score - new_peak)
    new_whole = whole * old_factor + own_factor

    def pick(values_full):
        return lax.dynamic_slice_in_dim(values_full, col_start, col_count, 1)

    new_sums = sums_part * pick(jnp.repeat(old_factor, HEAD_DIM, axis=1)) + pick(
        own_sums * jnp.repeat(own_factor, HEAD_DIM, axis=1)
    )
    attn_part = (new_sums / pick(jnp.repeat(new_whole, HEAD_DIM, axis=1))).astype(jnp.bfloat16)
    partial_value = jnp.dot(attn_part, w_out, preferred_element_type=jnp.float32)
    return lax.psum_scatter(partial_value, "tp", scatter_dimension=1, tiled=True).astype(
        jnp.bfloat16
    )


def solution(mesh):
    in_specs = (
        P("group", None),
        P(None, "tp"),
        P("tp", None),
        P(("group", "tp"), None, None),
        P(),
        P(),
    )
    out_specs = P("group", "tp")
    return jax.shard_map(
        on_device, mesh=mesh, in_specs=in_specs, out_specs=out_specs, check_vma=False
    )
```

profile of v0, /device:TPU:2, one launch (start us, length us, event | category | flops | bytes accessed | tf_op | source)
XLA Modules:
  0.0 429.0 jit_solution(9588263399593622062)
XLA Ops:
  6.5 0.0 copy-start
  6.5 0.0 copy-start.1
  6.5 0.0 all-reduce.2.cloned.1.call-start
  6.5 1.1 fusion.1
  7.6 0.1 iota_compare_fusion
  7.7 0.2 copy-done
  8.0 1.0 convolution_convert_fusion
  9.0 19.1 %all_gather.6 = bf16[2,2048]{1,0:T(2,128)(2,1)S(1)} all-gather(bf16[2,256]{1,0:T(2,128)(2,1)S(1)} %convolution_convert_fusion), channel_id=1, replica_groups=mesh['group'=32,'tp'=8] {'tp'}, dimensions={1}, use_global_device_ids=true | all-gather | bytes 9216 | tf_op jit(solution)/shard_map/all_gather | solution.py:20
  28.1 24.7 %all-gather = bf16[32,2,1536]{2,1,0:T(2,128)(2,1)S(1)} all-gather(bf16[1,2,1536]{2,1,0:T(2,128)(2,1)S(1)} %get-tuple-element.19), channel_id=1, replica_groups=mesh['group'=32,'tp'=8] {'group'}, dimensions={0}, use_global_device_ids=true | all-gather | bytes 202752 | tf_op jit(solution)/shard_map/all_gather | solution.py:21
  52.8 0.1 reshape.166
  52.9 0.0 copy-done.1
  52.9 0.6 gather_fusion
  53.5 0.6 gather_fusion.1
  54.1 1.3 fusion.25
  55.4 0.3 copy.96
  55.7 0.1 add_compare_fusion
  55.8 0.3 select_reduce_fusion
  56.1 0.1 copy.81
  56.2 0.1 select_reduce_fusion.1
  56.3 0.1 copy.82
  56.4 0.3 copy.97
  56.7 0.2 convert_reduce_fusion
  56.9 0.1 copy.86
  57.0 74.0 %pmax.7 = f32[64,12]{1,0:T(8,128)S(1)} all-reduce(f32[64,12]{1,0:T(8,128)S(1)} %copy.86), channel_id=1, replica_groups=mesh['group'=32,'tp'=8] {'group','tp'}, use_global_device_ids=true, to_apply=%region_4.5 | all-reduce | flops 768 | bytes 6144 | tf_op jit(solution)/shard_map/pmax | solution.py:58
  131.0 0.6 gather_fusion.2
  131.6 0.2 fusion.5
  131.8 0.1 copy.88
  131.9 0.4 convolution_multiply_fusion
  132.3 0.4 fusion.2
  132.8 0.2 copy.84
  133.0 0.1 reshape.129
  133.1 0.0 copy-start.2
  133.2 0.2 broadcast_in_dim.104
  133.4 0.9 bitcast_multiply_fusion
  134.3 0.0 all-reduce.2.cloned.1.call-update
  134.3 0.0 reduce-scatter.4.cloned.1.call-start
  134.4 0.1 fusion.27
  134.5 0.1 reshape.134
  134.6 74.9 %psum.15 = f32[64,12]{1,0:T(8,128)S(1)} all-reduce(f32[64,12]{1,0:T(8,128)S(1)} %get-tuple-element.10), channel_id=1, replica_groups=mesh['group'=32,'tp'=8] {'group','tp'}, use_global_device_ids=true, to_apply=%region_7.8 | all-reduce | flops 768 | bytes 6144 | tf_op jit(solution)/shard_map/psum | solution.py:60
  209.5 0.1 broadcast_bitcast_fusion.2
  209.6 0.1 broadcast_bitcast_fusion
  209.7 168.6 %all-reduce.2.cloned.1.call-done = f32[64,1536]{1,0:T(8,128)} async-done(((f32[64,1536]{1,0:T(8,128)}), f32[64,1536]{1,0:T(8,128)}) %all-reduce.2.cloned.1.call-update) | async-done | bytes 393232 | tf_op jit(solution)/shard_map/psum | solution.py:60
  378.3 0.0 copy-done.2
  378.3 2.7 convolution_bitcast_fusion
  381.0 0.0 reduce-scatter.4.cloned.1.call-update
  381.0 39.5 %reduce-scatter.4.cloned.1.call-done = f32[384,2]{1,0:T(8,128)} async-done(((f32[3072,2]{1,0:T(8,128)}), f32[384,2]{1,0:T(8,128)}) %reduce-scatter.4.cloned.1.call-update) | async-done | bytes 3088
  420.5 1.6 copy.95
  (20 shorter events, 0.2 us)
Async XLA Ops:
  6.5 1.4 copy-start
  6.5 46.4 %copy-start.1 = (s32[64]{0:T(128)S(1)}, s32[64]{0:T(128)}, u32[]{:S(2)}) copy-start(s32[64]{0:T(128)} %param.11) | copy-start | bytes 772
  6.5 371.7 %all-reduce.2.cloned.1.call-start = ((), (), s32[]{:S(2)}) async-start(), calls=%async_computation.1 | async-start | bytes 786432 | tf_op jit(solution)/shard_map/psum | solution.py:60
  133.1 245.2 %copy-start.2 = (bf16[192,3072]{1,0:T(8,128)(2,1)S(1)}, bf16[192,3072]{1,0:T(8,128)(2,1)}, u32[]{:S(2)}) copy-start(bf16[192,3072]{1,0:T(8,128)(2,1)} %param.8) | copy-start | bytes 3538948
  134.3 286.2 %reduce-scatter.4.cloned.1.call-start = ((), (), s32[]{:S(2)}) async-start(), calls=%async_computation.2 | async-start | bytes 1769472
Sparse Core Ops, SparseCore 0:
  134.4 243.8 all-reduce.1
  381.1 39.3 reduce-scatter.3
where the time goes:
time: 430 us; the launch traced here: 429 us
  waiting for transfers between devices  208 us (48%)
  blocking collectives  193 us (45%)
  between operations  13.6 us (3%)
  local copies, waits for them, and re-layouts  6.81 us (2%)
  matrix products  5.21 us (1%)
    psum x1, waiting for transfers between devices, on_device(): lax.psum((req_total * rescale, req_sums * jnp.repeat(rescale, HEAD_DIM, a...  169 us
    psum x1, blocking collectives, on_device(): lax.psum((req_total * rescale, req_sums * jnp.repeat(rescale, HEAD_DIM, a...  74.9 us
    pmax x1, blocking collectives, on_device(): peak_all = lax.pmax(req_top, ('group', 'tp'))  74 us
    unnamed x3, waiting for transfers between devices  39.6 us
    all_gather x1, blocking collectives, on_device(): queries = lax.all_gather(qkv[:, :qdim], 'group', axis=0, tiled=True)  24.7 us
    all_gather x1, blocking collectives, on_device(): qkv = lax.all_gather(columns, 'tp', axis=1, tiled=True)  19.1 us
  transfers between devices with their start and end apart: 2, of which 2 were waited for; matrix products, arithmetic and copies ran while one was open for 0% of the time, Pallas kernels for 0%

commit v1 on v0

--- a/solution.py
+++ b/solution.py
@@ -18,7 +18,9 @@
     col_start = lax.axis_index("tp") * col_count
     columns = jnp.dot(hidden_in, w_qkv, preferred_element_type=jnp.float32).astype(jnp.bfloat16)
     qkv = lax.all_gather(columns, "tp", axis=1, tiled=True)
-    queries = lax.all_gather(qkv[:, :qdim], "group", axis=0, tiled=True)
+    queries = jnp.concatenate(
+        lax.all_to_all(jnp.stack([qkv[:, :qdim]] * lax.axis_size("group")), "group", 0, 0), axis=0
+    )
     requests = queries.shape[0]
     slot_count = kv_pool.shape[0]
     page_len = kv_pool.shape[1]

time: 430 us -> 491 us (1.14)
  waiting for transfers between devices: 208 us -> 287 us
  blocking collectives: 193 us -> 167 us
  starting transfers between devices: 0.04 us -> 7.71 us
    psum x1, waiting for transfers between devices: 169 us -> 243 us  [on_device(): lax.psum((req_total * rescale, req_sums * jnp.repeat(rescale, HEAD_DIM, a...]
    all_gather x1 -> x0, blocking collectives: 24.7 us -> none  [on_device(): queries = lax.all_gather(qkv[:, :qdim], 'group', axis=0, tiled=True)]
    all_to_all x0 -> x1, starting transfers between devices: none -> 7.62 us  [on_device(): lax.all_to_all(jnp.stack([qkv[:, :qdim]] * lax.axis_size('group')), 'grou...]
  transfers between devices with their start and end apart: 2 -> 3, of which waited for: 2 -> 3; matrix products, arithmetic and copies ran while one was open for 0% -> 1% of each run, Pallas kernels for 0% -> 0%
where the time goes in v1:
time: 491 us; the launch traced here: 490 us
  waiting for transfers between devices  287 us (58%)
  blocking collectives  167 us (34%)
  between operations  13.6 us (3%)
  local copies, waits for them, and re-layouts  8.81 us (2%)
  starting transfers between devices  7.71 us (2%)
  matrix products  5.19 us (1%)
    psum x1, waiting for transfers between devices, on_device(): lax.psum((req_total * rescale, req_sums * jnp.repeat(rescale, HEAD_DIM, a...  243 us
    psum x1, blocking collectives, on_device(): lax.psum((req_total * rescale, req_sums * jnp.repeat(rescale, HEAD_DIM, a...  74.5 us
    pmax x1, blocking collectives, on_device(): peak_all = lax.pmax(req_top, ('group', 'tp'))  73.4 us
    unnamed x3, waiting for transfers between devices  39.6 us
    all_gather x1, blocking collectives, on_device(): qkv = lax.all_gather(columns, 'tp', axis=1, tiled=True)  19.1 us
  transfers between devices with their start and end apart: 3, of which 3 were waited for; matrix products, arithmetic and copies ran while one was open for 1% of the time, Pallas kernels for 0%

profile of v1, /device:TPU:2, one launch (start us, length us, event | category | flops | bytes accessed | tf_op | source)
XLA Modules:
  0.0 490.4 jit_solution(3824054482936572742)
XLA Ops:
  6.5 0.0 copy-start
  6.5 1.4 copy-done
  7.9 1.0 convolution_convert_fusion
  9.0 19.1 %all_gather.3 = bf16[2,2048]{1,0:T(2,128)(2,1)S(1)} all-gather(bf16[2,256]{1,0:T(2,128)(2,1)S(1)} %convolution_convert_fusion), channel_id=1, replica_groups=mesh['group'=32,'tp'=8] {'tp'}, dimensions={1}, use_global_device_ids=true | all-gather | bytes 9216 | tf_op jit(solution)/shard_map/all_gather | solution.py:20
  28.1 0.8 stack.2
  28.9 7.6 %all-to-all-start = ((bf16[32,2,1536]{2,1,0:T(2,128)(2,1)}), bf16[32,2,1536]{2,1,0:T(2,128)(2,1)S(1)}, u32[]{:S(2)}, u32[]{:S(2)}) async-start(bf16[32,2,1536]{2,1,0:T(2,128)(2,1)} %stack.2), calls=%async_computation | async-start | bytes 393216 | tf_op jit(solution)/shard_map/all_to_all | solution.py:22
  36.5 0.0 all-reduce.2.cloned.1.call-start
  36.6 0.2 fusion.1
  36.9 0.1 fusion.26
  37.0 0.1 reshape.140
  37.1 1.3 fusion.25
  38.4 0.0 copy-start.1
  38.4 0.3 copy.97
  38.7 0.3 copy.96
  39.0 0.1 copy-done.1
  39.1 0.6 gather_fusion
  39.7 0.1 add_compare_fusion
  39.8 0.1 iota_compare_fusion
  39.9 3.8 all-to-all-done
  43.6 0.1 reshape.131
  43.7 0.6 gather_fusion.1
  44.3 0.3 select_reduce_fusion
  44.6 0.1 copy.81
  44.7 0.1 select_reduce_fusion.1
  44.8 0.1 copy.82
  45.0 0.2 convert_reduce_fusion
  45.1 0.1 copy.86
  45.2 73.4 %pmax.7 = f32[64,12]{1,0:T(8,128)S(1)} all-reduce(f32[64,12]{1,0:T(8,128)S(1)} %copy.86), channel_id=1, replica_groups=mesh['group'=32,'tp'=8] {'group','tp'}, use_global_device_ids=true, to_apply=%region_4.5 | all-reduce | flops 768 | bytes 6144 | tf_op jit(solution)/shard_map/pmax | solution.py:60
  118.6 0.6 gather_fusion.2
  119.2 0.2 fusion.5
  119.4 0.1 copy.88
  119.5 74.5 %psum.15 = f32[64,12]{1,0:T(8,128)S(1)} all-reduce(f32[64,12]{1,0:T(8,128)S(1)} %get-tuple-element.10), channel_id=1, replica_groups=mesh['group'=32,'tp'=8] {'group','tp'}, use_global_device_ids=true, to_apply=%region_7.8 | all-reduce | flops 768 | bytes 6144 | tf_op jit(solution)/shard_map/psum | solution.py:62
  194.0 0.1 broadcast_bitcast_fusion.2
  194.1 0.4 convolution_multiply_fusion
  194.5 0.4 fusion.2
  194.9 0.2 copy.84
  195.2 0.1 reshape.135
  195.3 0.0 copy-start.2
  195.3 0.2 broadcast_in_dim.104
  195.5 0.9 bitcast_multiply_fusion
  196.4 0.0 all-reduce.2.cloned.1.call-update
  196.4 0.0 reduce-scatter.4.cloned.1.call-start
  196.5 0.1 broadcast_bitcast_fusion
  196.6 243.2 %all-reduce.2.cloned.1.call-done = f32[64,1536]{1,0:T(8,128)} async-done(((f32[64,1536]{1,0:T(8,128)}), f32[64,1536]{1,0:T(8,128)}) %all-reduce.2.cloned.1.call-update) | async-done | bytes 393232 | tf_op jit(solution)/shard_map/psum | solution.py:62
  439.8 2.7 convolution_bitcast_fusion
  442.4 0.0 reduce-scatter.4.cloned.1.call-update
  442.5 39.5 %reduce-scatter.4.cloned.1.call-done = f32[384,2]{1,0:T(8,128)} async-done(((f32[3072,2]{1,0:T(8,128)}), f32[384,2]{1,0:T(8,128)}) %reduce-scatter.4.cloned.1.call-update) | async-done | bytes 3088
  482.0 1.6 copy.95
  (23 shorter events, 0.2 us)
Async XLA Ops:
  6.5 1.4 copy-start
  6.5 30.1 %copy-start.3 = (s32[64,32]{0,1:T(8,128)S(1)}, s32[64,32]{0,1:T(8,128)}, u32[]{:S(2)}) copy-start(s32[64,32]{0,1:T(8,128)} %param.10) | copy-start | bytes 24580
  28.9 14.8 %all-to-all-start = ((bf16[32,2,1536]{2,1,0:T(2,128)(2,1)}), bf16[32,2,1536]{2,1,0:T(2,128)(2,1)S(1)}, u32[]{:S(2)}, u32[]{:S(2)}) async-start(bf16[32,2,1536]{2,1,0:T(2,128)(2,1)} %stack.2), calls=%async_computation | async-start | bytes 393216 | tf_op jit(solution)/shard_map/all_to_all | solution.py:22
  36.5 403.2 %all-reduce.2.cloned.1.call-start = ((), (), s32[]{:S(2)}) async-start(), calls=%async_computation.2 | async-start | bytes 786432 | tf_op jit(solution)/shard_map/psum | solution.py:62
  38.4 0.7 copy-start.1
  195.3 244.5 %copy-start.2 = (bf16[192,3072]{1,0:T(8,128)(2,1)S(1)}, bf16[192,3072]{1,0:T(8,128)(2,1)}, u32[]{:S(2)}) copy-start(bf16[192,3072]{1,0:T(8,128)(2,1)} %param.8) | copy-start | bytes 3538948
  196.4 285.6 %reduce-scatter.4.cloned.1.call-start = ((), (), s32[]{:S(2)}) async-start(), calls=%async_computation.3 | async-start | bytes 1769472
Sparse Core Ops, SparseCore 0:
  196.6 243.1 all-reduce.1
  442.6 39.3 reduce-scatter.3
